TPU v7x, 256 devices: a whole 4x4x8 slice. The times are simulated.
256 devices in a mesh: cfg: 2 (over core), seq: 32 (over y, z), blk: 4 (over x).
Axes of the slice: x: 4, y: 4, z: 8, core: 2. Of those that a mesh axis runs over, the one named last changes fastest.
Arguments:
- queries: bfloat16 [2, 12288, 1536], P('cfg', 'seq', 'blk'), may hold values from -20 to 20
- keys: bfloat16 [2, 12288, 1536], P('cfg', 'seq', 'blk'), may hold values from -20 to 20
- values: bfloat16 [2, 12288, 1536], P('cfg', 'seq', 'blk'), may hold values from -6 to 6
- residual: bfloat16 [2, 12288, 1536], P('cfg', 'seq'), may hold values from -6 to 6
- w_out: bfloat16 [1536, 1536], P('blk'), may hold values from -0.15625 to 0.15625
- w_up: bfloat16 [1536, 6144], P(None, 'blk'), may hold values from -0.15625 to 0.15625
- w_down: bfloat16 [6144, 1536], P('blk'), may hold values from -0.078125 to 0.078125
- modulation: float32 [3, 4, 1536], replicated, may hold values from -3 to 3
- guide_scale: float32 [3], replicated, may hold values from 1.5 to 4
- slot_clip: int32 [12288], P('seq'), may hold values from 0 to 3, as said below
- owner: int32 [12288, 1], P('seq'), may hold values from 0 to 31; in each aligned block of 192 rows (0 to 191, 192 to 383, ...) at most 12 rows name the same one
Outputs:
- returned: bfloat16 [2, 12288, 1536], P('cfg', 'seq', 'blk')
Inputs may be any that keep to these rules, and one draw needn't show every extreme that they name: `slot_clip`: each device's block of 384 slots holds its live slots first and its padding slots, marked 3, last; live slots, counted block after block, are dealt to the clips in turn (the t-th live slot belongs to clip t mod 3), so each clip has 3584 live slots. In each aligned half-block of 192 slots no owner is named more than 12 times.
All inputs are finite; a program needn't handle non-finite values.
Results may differ from a plain program's by a relative error of at most 0.017.
Values may be sent and summed in bfloat16 or wider, within the bound.
A program may use at most 128 MiB of HBM per device.

v0:
```python
import math
import jax
import jax.numpy as jnp
from jax import lax
from jax.sharding import PartitionSpec as P

D = 1536
HEAD_DIM = 128
CLIPS = 3
NEG_FILL = -1e30


def swapped(value, axis, bit):
    mask = 2**bit
    pairs = [(source, source ^ mask) for source in range(lax.axis_size(axis))]
    return lax.ppermute(value, axis, pairs)


def shards(
    queries, keys, values, residual, w_out, w_up, w_down, modulation, guide_scale, slot_clip, owner
):
    query_here = queries[0]
    slots, width = query_here.shape
    heads_here = width // HEAD_DIM
    factor = 1.0 / math.sqrt(HEAD_DIM)
    live = slot_clip < CLIPS
    query_heads = query_here.reshape(slots, heads_here, HEAD_DIM)

    def absorb_block(carry, key_block, value_block, clip_block):
        count = key_block.shape[0]
        kept = (clip_block[None, :] == slot_clip[:, None]) & live[:, None]
        best, total, accum = carry
        key_heads = key_block.reshape(count, heads_here, HEAD_DIM)
        value_heads = value_block.reshape(count, heads_here, HEAD_DIM)
        scores = (
            jnp.einsum("qhd,khd->hqk", query_heads, key_heads, preferred_element_type=jnp.float32)
            * factor
        )
        scores = jnp.where(kept[None], scores, NEG_FILL)
        new_best = jnp.maximum(best, jnp.max(scores, axis=-1))
        fade = jnp.exp(best - new_best)
        probs = jnp.exp(scores - new_best[..., None])
        total = total * fade + jnp.sum(probs, axis=-1)
        added = jnp.einsum(
            "hqk,khd->qhd",
            probs.astype(jnp.bfloat16),
            value_heads,
            preferred_element_type=jnp.float32,
        )
        accum = accum * jnp.transpose(fade)[:, :, None] + added
        return (new_best, total, accum)

    def absorb(carry, piece):
        key_piece, value_piece, clip_piece = piece
        count = key_piece.shape[0]
        step_rows = next(
            (size_b for size_b in (512, 384, 256, 128) if count % size_b == 0 and count > size_b),
            count,
        )
        if step_rows == count:
            return absorb_block(carry, key_piece, value_piece, clip_piece)
        blocks = count // step_rows

        def scan_step(state, block_items):
            return (absorb_block(state, block_items[0], block_items[1], block_items[2]), None)

        stacked = (
            key_piece.reshape(blocks, step_rows, width),
            value_piece.reshape(blocks, step_rows, width),
            clip_piece.reshape(blocks, step_rows),
        )
        carry_out, unused = lax.scan(scan_step, carry, stacked)
        return carry_out

    start_state = (
        jnp.full((heads_here, slots), NEG_FILL, jnp.float32),
        jnp.zeros((heads_here, slots), jnp.float32),
        jnp.zeros((slots, heads_here, HEAD_DIM), jnp.float32),
    )
    best, total, accum = absorb(
        start_state,
        (
            lax.all_gather(keys[0], "seq", axis=0, tiled=True),
            lax.all_gather(values[0], "seq", axis=0, tiled=True),
            lax.all_gather(slot_clip, "seq", axis=0, tiled=True),
        ),
    )
    attended = (accum / jnp.transpose(total)[:, :, None]).reshape(slots, width)
    attended = jnp.where(live[:, None], attended, 0.0).astype(jnp.bfloat16)
    partial_out = jnp.dot(attended, w_out, preferred_element_type=jnp.float32)
    selector = (slot_clip[:, None] == jnp.arange(CLIPS, dtype=jnp.int32)[None, :]).astype(
        jnp.float32
    )
    row_mod = jnp.dot(
        selector, modulation.reshape(CLIPS, 4 * D), precision=lax.Precision.HIGHEST
    ).reshape(slots, 4, D)
    columns = D // lax.axis_size("blk")
    col_start = lax.axis_index("blk") * columns
    mod_cols = lax.dynamic_slice_in_dim(row_mod, col_start, columns, 2)
    projected = lax.psum(partial_out.astype(jnp.bfloat16), "blk").astype(jnp.float32)
    mixed = residual[0].astype(jnp.float32) + row_mod[:, 0] * projected
    centre = mixed - jnp.mean(mixed, axis=-1, keepdims=True)
    spread = jnp.mean(centre * centre, axis=-1, keepdims=True)
    normed = (centre * lax.rsqrt(spread + 1e-06) * (1.0 + row_mod[:, 2]) + row_mod[:, 1]).astype(
        jnp.bfloat16
    )
    mixed_cols = lax.dynamic_slice_in_dim(mixed, col_start, columns, 1)
    hidden = jax.nn.gelu(
        jnp.dot(normed, w_up, preferred_element_type=jnp.float32), approximate=True
    ).astype(jnp.bfloat16)
    terms = jnp.dot(hidden, w_down, preferred_element_type=jnp.float32)
    summed = lax.psum_scatter(
        terms.astype(jnp.bfloat16), "blk", scatter_dimension=1, tiled=True
    ).astype(jnp.float32)
    block_out = (mixed_cols + mod_cols[:, 3] * summed).astype(jnp.bfloat16)
    half_len = slots // 2
    side = lax.axis_index("cfg")
    partner = swapped(block_out, "cfg", 0)
    cond_all = jnp.where(side == 0, block_out, partner)
    uncond_all = jnp.where(side == 0, partner, block_out)
    cond_rows = lax.dynamic_slice_in_dim(cond_all, side * half_len, half_len, 0)
    uncond_rows = lax.dynamic_slice_in_dim(uncond_all, side * half_len, half_len, 0)
    clip_half = lax.dynamic_slice_in_dim(slot_clip, side * half_len, half_len, 0)
    clip_pick = (clip_half[:, None] == jnp.arange(CLIPS, dtype=jnp.int32)[None, :]).astype(
        jnp.float32
    )
    strength = jnp.sum(clip_pick * guide_scale[None, :], axis=1)
    cond_float = cond_rows.astype(jnp.float32)
    uncond_float = uncond_rows.astype(jnp.float32)
    guided = uncond_float + strength[:, None] * (cond_float - uncond_float)
    guided = jnp.where((clip_half < CLIPS)[:, None], guided, 0.0).astype(jnp.bfloat16)
    seq_count = lax.axis_size("seq")
    capacity = max(2, slots // seq_count)
    owner_half = lax.dynamic_slice_in_dim(owner[:, 0], side * half_len, half_len, 0)
    owner_hot = (owner_half[:, None] == jnp.arange(seq_count, dtype=jnp.int32)[None, :]).astype(
        jnp.int32
    )
    rank = jnp.sum((jnp.cumsum(owner_hot, axis=0) - owner_hot) * owner_hot, axis=1)
    target = owner_half * capacity + rank
    placing = (
        jnp.arange(seq_count * capacity, dtype=jnp.int32)[:, None] == target[None, :]
    ).astype(jnp.bfloat16)
    outgoing = jnp.dot(placing, guided, preferred_element_type=jnp.float32).astype(jnp.bfloat16)
    outgoing = outgoing.reshape(seq_count, capacity, columns)
    arrived = lax.all_to_all(outgoing, "seq", split_axis=0, concat_axis=0, tiled=True)
    return arrived.reshape(1, seq_count * capacity, columns)


def solution(mesh):
    placed = (
        P("cfg", "seq", "blk"),
        P("cfg", "seq", "blk"),
        P("cfg", "seq", "blk"),
        P("cfg", "seq", None),
        P("blk", None),
        P(None, "blk"),
        P("blk", None),
        P(),
        P(),
        P("seq"),
        P("seq", None),
    )
    return jax.shard_map(
        shards, mesh=mesh, in_specs=placed, out_specs=P("cfg", "seq", "blk"), check_vma=False
    )
```

profile of v0, /device:TPU:32, one launch (start us, length us, event | category | flops | bytes accessed | tf_op | source)
XLA Modules:
  0.0 713.3 jit_solution(6214231156440288934)
XLA Ops:
  10.8 48.8 %all-gather.2 = s32[32,1,384]{2,1,0:T(1,128)S(1)} all-gather(s32[1,1,384]{2,1,0:T(1,128)S(1)} %reshape.132), channel_id=1, replica_groups=mesh['cfg'=2,'seq'=32,'blk'=4] {'seq'}, dimensions={0}, use_global_device_ids=true | all-gather | bytes 50688 | tf_op jit(solution)/shard_map/all_gather | solution.py:85
  61.6 53.0 %all-gather.6.cloned.1.call-done = bf16[1,12288,384]{2,1,0:T(8,128)(2,1)} async-done(((bf16[1,384,384]{2,1,0:T(8,128)(2,1)}), bf16[1,12288,384]{2,1,0:T(8,128)(2,1)}) %all-gather.6.cloned.1.call-update) | async-done | bytes 9437200 | tf_op jit(solution)/shard_map/all_gather | solution.py:83
  114.6 103.2 %all-gather.8.cloned.1.call-done = bf16[1,12288,384]{2,1,0:T(8,128)(2,1)} async-done(((bf16[1,384,384]{2,1,0:T(8,128)(2,1)}), bf16[1,12288,384]{2,1,0:T(8,128)(2,1)}) %all-gather.8.cloned.1.call-update) | async-done | bytes 9437200 | tf_op jit(solution)/shard_map/all_gather | solution.py:84
  217.8 360.1 %while.15 = (s32[]{:T(128)}, f32[3,384]{1,0:T(4,128)S(1)}, f32[3,384]{1,0:T(4,128)}, f32[384,3,128]{0,2,1:T(8,128)}, s32[24,512]{1,0:T(8,128)}, /*index=5*/s32[3...) while((s32[]{:T(128)}, f32[3,384]{1,0:T(4,128)S(1)}, ...), condition=%wide.region_6.7_spmd.clone, body=%wide.region_3.6_spmd.clone.sunk | while | flops 309320448 | bytes 14176349 | solution.py:72
  243.4 2.9 fusion.94
  258.4 2.9 fusion.94
  273.4 2.9 fusion.94
  288.4 2.9 fusion.94
  303.4 2.9 fusion.94
  318.5 2.9 fusion.94
  333.5 2.9 fusion.94
  348.5 2.9 fusion.94
  363.5 2.9 fusion.94
  378.5 2.9 fusion.94
  393.5 2.9 fusion.94
  423.6 2.9 fusion.94
  438.6 2.9 fusion.94
  513.7 2.9 fusion.94
  528.7 2.9 fusion.94
  581.7 6.4 fusion.56
  588.2 44.1 %all-reduce.3.cloned.1.call-done = bf16[384,1536]{1,0:T(8,128)(2,1)} async-done(((bf16[384,1536]{1,0:T(8,128)(2,1)}), bf16[384,1536]{1,0:T(8,128)(2,1)}) %all-reduce.3.cloned.1.call-update) | async-done | bytes 1179664 | tf_op jit(solution)/shard_map/psum | solution.py:100
  635.4 10.1 %convolution_convert_fusion = bf16[384,1536]{1,0:T(8,128)(2,1)} fusion(bf16[1536,1536]{1,0:T(8,128)(2,1)} %param.19, bf16[1536,1536]{1,0:T(8,128)(2,1)} %param.18, f32[384,4,1536]{2,0,1:T(8,128)} %fusion.56, f32[384,1536]{1,0:T(8,128)S(1)} %get-tuple-element.158, f32[384]{0:T(512)S(1)} %add_rsqrt_fusion, f32[384]{0:T(512)S(1)} %broadcast_multiply_fusion), kind=kOutput, calls=%fused_computation.24 | convolution fusion | flops 3633315840 | bytes 17697792 | tf_op jit(solution)/shard_map/dot_general | solution.py:111
  652.9 22.6 %reduce-scatter.4.cloned.1.call-done = bf16[384,384]{1,0:T(8,128)(2,1)} async-done(((bf16[1536,384]{1,0:T(8,128)(2,1)}), bf16[384,384]{1,0:T(8,128)(2,1)}) %reduce-scatter.4.cloned.1.call-update) | async-done | bytes 294928
  680.8 25.2 %all_to_all.5 = bf16[32,12,384]{2,1,0:T(8,128)(2,1)S(1)} all-to-all(bf16[32,12,384]{2,1,0:T(8,128)(2,1)S(1)} %reshape.124), channel_id=1, replica_groups=mesh['cfg'=2,'seq'=32,'blk'=4] {'seq'}, dimensions={0} | all-to-all | bytes 589824 | tf_op jit(solution)/shard_map/all_to_all | solution.py:145
  (447 shorter events, 342.7 us)
Async XLA Ops:
  6.5 573.2 %copy-start = (bf16[384,1536]{1,0:T(8,128)(2,1)S(1)}, bf16[384,1536]{1,0:T(8,128)(2,1)}, u32[]{:S(2)}) copy-start(bf16[384,1536]{1,0:T(8,128)(2,1)} %param.17) | copy-start | bytes 3538948
  6.5 108.1 %all-gather.6.cloned.1.call-start = ((), (), s32[]{:S(2)}) async-start(), calls=%async_computation.3 | async-start | bytes 9732096 | tf_op jit(solution)/shard_map/all_gather | solution.py:83
  7.3 210.5 %all-gather.8.cloned.1.call-start = ((), (), s32[]{:S(2)}) async-start(), calls=%async_computation.4 | async-start | bytes 9732096 | tf_op jit(solution)/shard_map/all_gather | solution.py:84
  8.0 624.2 %all-reduce.3.cloned.1.call-start = ((), (), s32[]{:S(2)}) async-start(), calls=%async_computation.2 | async-start | bytes 2359296 | tf_op jit(solution)/shard_map/psum | solution.py:100
  243.4 2.9 copy-start.1
  258.4 2.9 copy-start.1
  273.4 2.9 copy-start.1
  288.4 2.9 copy-start.1
  303.4 2.9 copy-start.1
  318.5 2.9 copy-start.1
  333.5 2.9 copy-start.1
  348.5 2.9 copy-start.1
  363.5 2.9 copy-start.1
  378.5 2.9 copy-start.1
  393.5 2.9 copy-start.1
  408.5 2.9 copy-start.1
  423.6 2.9 copy-start.1
  438.6 2.9 copy-start.1
  453.6 2.9 copy-start.1
  468.6 2.9 copy-start.1
  483.6 2.9 copy-start.1
  581.6 93.9 %reduce-scatter.4.cloned.1.call-start = ((), (), s32[]{:S(2)}) async-start(), calls=%async_computation.5 | async-start | bytes 1474560
  652.9 27.4 %copy-start.7 = (pred[192]{0:T(512)(128)(4,1)S(1)}, pred[192]{0:T(512)(128)(4,1)}, u32[]{:S(2)}) copy-start(pred[192]{0:T(512)(128)(4,1)} %get-tuple-element.155) | copy-start | bytes 580
  678.7 1.7 collective-permute-start
  (58 other events, 58.8 us)
Sparse Core Ops, SparseCore 0:
  9.9 104.6 all-gather.5
  117.2 100.5 all-gather.7
  581.8 50.4 all-reduce.2
  648.0 27.5 reduce-scatter.3
where the time goes:
time: 720 us; the launch traced here: 713 us
  waiting for transfers between devices  225 us (31%)
  local copies, waits for them, and re-layouts  160 us (22%)
  matrix products  146 us (20%)
  other arithmetic  94.2 us (13%)
  blocking collectives  74 us (10%)
  between operations  13.3 us (2%)
    dynamic_slice x96, local copies, waits for them, and re-layouts, absorb(): carry_out, unused = lax.scan(scan_step, carry, stacked)  133 us
    all_gather x1, waiting for transfers between devices, shards(): lax.all_gather(values[0], 'seq', axis=0, tiled=True)  103 us
    dot_general x24, matrix products, absorb_block(): jnp.einsum('hqk,khd->qhd', probs.astype(jnp.bfloat16), value_heads, prefe...  69.4 us
    dot_general x24, matrix products, absorb_block(): jnp.einsum('qhd,khd->hqk', query_heads, key_heads, preferred_element_type...  57.5 us
    all_gather x1, waiting for transfers between devices, shards(): lax.all_gather(keys[0], 'seq', axis=0, tiled=True)  53 us
    all_gather x1, blocking collectives, shards(): lax.all_gather(slot_clip, 'seq', axis=0, tiled=True)  48.8 us
    psum x1, waiting for transfers between devices, shards(): lax.psum(partial_out.astype(jnp.bfloat16), 'blk').astype(jnp.float32)  44.1 us
    and x24, other arithmetic, absorb_block(): kept = (clip_block[None, :] == slot_clip[:, None]) & live[:, None]  37.3 us
  transfers between devices with their start and end apart: 5, of which 5 were waited for; matrix products, arithmetic and copies ran while one was open for 2% of the time, Pallas kernels for 0%

commit v1 on v0

--- a/solution.py
+++ b/solution.py
@@ -81,7 +81,9 @@
         start_state,
         (
             lax.all_gather(keys[0], "seq", axis=0, tiled=True),
-            lax.all_gather(values[0], "seq", axis=0, tiled=True),
+            jnp.concatenate(
+                lax.all_to_all(jnp.stack([values[0]] * lax.axis_size("seq")), "seq", 0, 0), axis=0
+            ),
             lax.all_gather(slot_clip, "seq", axis=0, tiled=True),
         ),
     )

time: 720 us -> 834 us (1.16)
  blocking collectives: 74 us -> 326 us
  waiting for transfers between devices: 225 us -> 69.1 us
  starting transfers between devices: 0.21 us -> 11.9 us
    all_gather x1, blocking collectives: 48.8 us -> 301 us  [shards(): lax.all_gather(slot_clip, 'seq', axis=0, tiled=True)]
    all_gather x1 -> x0, waiting for transfers between devices: 103 us -> none  [shards(): lax.all_gather(values[0], 'seq', axis=0, tiled=True)]
    all_gather x1, waiting for transfers between devices: 53 us -> 0.01 us  [shards(): lax.all_gather(keys[0], 'seq', axis=0, tiled=True)]
    all_to_all x0 -> x1, starting transfers between devices: none -> 11.5 us  [shards(): lax.all_to_all(jnp.stack([values[0]] * lax.axis_size('seq')), 'seq', 0, 0)]
    unnamed x5 -> x4, waiting for transfers between devices: 24.1 us -> 22.7 us
  transfers between devices with their start and end apart: 5 -> 5, of which waited for: 5 -> 3; matrix products, arithmetic and copies ran while one was open for 2% -> 2% of each run, Pallas kernels for 0% -> 0%
where the time goes in v1:
time: 834 us; the launch traced here: 827 us
  blocking collectives  326 us (39%)
  local copies, waits for them, and re-layouts  165 us (20%)
  matrix products  147 us (18%)
  other arithmetic  95 us (11%)
  waiting for transfers between devices  69.1 us (8%)
  between operations  13.3 us (2%)
  starting transfers between devices  11.9 us (1%)
    all_gather x1, blocking collectives, shards(): lax.all_gather(slot_clip, 'seq', axis=0, tiled=True)  301 us
    dynamic_slice x96, local copies, waits for them, and re-layouts, absorb(): carry_out, unused = lax.scan(scan_step, carry, stacked)  133 us
    dot_general x24, matrix products, absorb_block(): jnp.einsum('hqk,khd->qhd', probs.astype(jnp.bfloat16), value_heads, prefe...  69.1 us
    dot_general x24, matrix products, absorb_block(): jnp.einsum('qhd,khd->hqk', query_heads, key_heads, preferred_element_type...  57.6 us
    psum x1, waiting for transfers between devices, shards(): lax.psum(partial_out.astype(jnp.bfloat16), 'blk').astype(jnp.float32)  45.6 us
    and x24, other arithmetic, absorb_block(): kept = (clip_block[None, :] == slot_clip[:, None]) & live[:, None]  37.6 us
    transpose x24, other arithmetic, absorb_block(): accum = accum * jnp.transpose(fade)[:, :, None] + added  31 us
    all_to_all x1, blocking collectives, shards(): lax.all_to_all(outgoing, 'seq', split_axis=0, concat_axis=0, tiled=True)  25.2 us
  transfers between devices with their start and end apart: 5, of which 3 were waited for; matrix products, arithmetic and copies ran while one was open for 2% of the time, Pallas kernels for 0%

profile of v1, /device:TPU:32, one launch (start us, length us, event | category | flops | bytes accessed | tf_op | source)
XLA Modules:
  0.0 827.5 jit_solution(2736977308631086339)
XLA Ops:
  6.5 6.2 stack.3
  12.7 11.5 %all-to-all-start = ((bf16[32,384,384]{2,1,0:T(8,128)(2,1)}), bf16[32,384,384]{2,1,0:T(8,128)(2,1)}, u32[]{:S(2)}, u32[]{:S(2)}) async-start(bf16[32,384,384]{2,1,0:T(8,128)(2,1)} %stack.3), calls=%async_computation | async-start | bytes 18874368 | tf_op jit(solution)/shard_map/all_to_all | solution.py:85
  26.9 300.7 %all-gather.1 = s32[32,1,384]{2,1,0:T(1,128)S(1)} all-gather(s32[1,1,384]{2,1,0:T(1,128)S(1)} %reshape.127), channel_id=1, replica_groups=mesh['cfg'=2,'seq'=32,'blk'=4] {'seq'}, dimensions={0}, use_global_device_ids=true | all-gather | bytes 50688 | tf_op jit(solution)/shard_map/all_gather | solution.py:87
  329.5 359.7 %while.15 = (s32[]{:T(128)}, f32[3,384]{1,0:T(4,128)S(1)}, f32[3,384]{1,0:T(4,128)}, f32[384,3,128]{0,2,1:T(8,128)}, s32[24,512]{1,0:T(8,128)}, /*index=5*/s32[3...) while((s32[]{:T(128)}, f32[3,384]{1,0:T(4,128)S(1)}, ...), condition=%wide.region_6.7_spmd.clone, body=%wide.region_3.6_spmd.clone.sunk | while | flops 309320448 | bytes 14176349 | solution.py:72
  370.1 2.9 fusion.94
  385.1 2.9 fusion.94
  400.1 2.9 fusion.94
  415.1 2.9 fusion.94
  430.1 2.9 fusion.94
  460.0 2.9 fusion.94
  475.0 2.9 fusion.94
  490.0 2.9 fusion.94
  520.0 2.9 fusion.94
  535.0 2.9 fusion.94
  550.0 2.9 fusion.94
  595.0 2.9 fusion.94
  610.0 2.9 fusion.94
  655.0 2.9 fusion.94
  670.0 2.9 fusion.94
  693.1 7.1 fusion.56
  700.3 45.6 %all-reduce.3.cloned.1.call-done = bf16[384,1536]{1,0:T(8,128)(2,1)} async-done(((bf16[384,1536]{1,0:T(8,128)(2,1)}), bf16[384,1536]{1,0:T(8,128)(2,1)}) %all-reduce.3.cloned.1.call-update) | async-done | bytes 1179664 | tf_op jit(solution)/shard_map/psum | solution.py:102
  749.0 10.1 %convolution_convert_fusion = bf16[384,1536]{1,0:T(8,128)(2,1)} fusion(bf16[1536,1536]{1,0:T(8,128)(2,1)} %param.19, bf16[1536,1536]{1,0:T(8,128)(2,1)} %param.18, f32[384,4,1536]{2,0,1:T(8,128)} %fusion.56, f32[384,1536]{1,0:T(8,128)S(1)} %get-tuple-element.158, f32[384]{0:T(512)S(1)} %add_rsqrt_fusion, f32[384]{0:T(512)S(1)} %broadcast_multiply_fusion), kind=kOutput, calls=%fused_computation.24 | convolution fusion | flops 3633315840 | bytes 17697792 | tf_op jit(solution)/shard_map/dot_general | solution.py:113
  767.2 22.0 %reduce-scatter.4.cloned.1.call-done = bf16[384,384]{1,0:T(8,128)(2,1)} async-done(((bf16[1536,384]{1,0:T(8,128)(2,1)}), bf16[384,384]{1,0:T(8,128)(2,1)}) %reduce-scatter.4.cloned.1.call-update) | async-done | bytes 294928
  795.0 25.2 %all_to_all.10 = bf16[32,12,384]{2,1,0:T(8,128)(2,1)S(1)} all-to-all(bf16[32,12,384]{2,1,0:T(8,128)(2,1)S(1)} %reshape.121), channel_id=1, replica_groups=mesh['cfg'=2,'seq'=32,'blk'=4] {'seq'}, dimensions={0} | all-to-all | bytes 589824 | tf_op jit(solution)/shard_map/all_to_all | solution.py:147
  (445 shorter events, 342.2 us)
Async XLA Ops:
  6.5 684.5 %copy-start = (bf16[384,1536]{1,0:T(8,128)(2,1)S(1)}, bf16[384,1536]{1,0:T(8,128)(2,1)}, u32[]{:S(2)}) copy-start(bf16[384,1536]{1,0:T(8,128)(2,1)} %param.17) | copy-start | bytes 3538948
  12.7 12.4 %copy-start.2 = (bf16[1,384,384]{2,1,0:T(8,128)(2,1)S(1)}, bf16[1,384,384]{2,1,0:T(8,128)(2,1)}, u32[]{:S(2)}) copy-start(bf16[1,384,384]{2,1,0:T(8,128)(2,1)} %param.13) | copy-start | bytes 884740
  12.7 316.8 %all-to-all-start = ((bf16[32,384,384]{2,1,0:T(8,128)(2,1)}), bf16[32,384,384]{2,1,0:T(8,128)(2,1)}, u32[]{:S(2)}, u32[]{:S(2)}) async-start(bf16[32,384,384]{2,1,0:T(8,128)(2,1)} %stack.3), calls=%async_computation | async-start | bytes 18874368 | tf_op jit(solution)/shard_map/all_to_all | solution.py:85
  24.3 305.2 %all-gather.4.cloned.1.call-start = ((), (), s32[]{:S(2)}) async-start(), calls=%async_computation.4 | async-start | bytes 9732096 | tf_op jit(solution)/shard_map/all_gather | solution.py:83
  25.0 720.8 %all-reduce.3.cloned.1.call-start = ((), (), s32[]{:S(2)}) async-start(), calls=%async_computation.3 | async-start | bytes 2359296 | tf_op jit(solution)/shard_map/psum | solution.py:102
  370.1 2.9 copy-start.1
  385.1 2.9 copy-start.1
  400.1 2.9 copy-start.1
  415.1 2.9 copy-start.1
  430.1 2.9 copy-start.1
  445.0 2.9 copy-start.1
  460.0 2.9 copy-start.1
  475.0 2.9 copy-start.1
  490.0 2.9 copy-start.1
  505.0 2.9 copy-start.1
  550.0 2.9 copy-start.1
  565.0 2.9 copy-start.1
  580.0 2.9 copy-start.1
  610.0 2.9 copy-start.1
  625.0 2.9 copy-start.1
  640.0 2.9 copy-start.1
  685.0 2.9 copy-start.1
  692.9 96.3 %reduce-scatter.4.cloned.1.call-start = ((), (), s32[]{:S(2)}) async-start(), calls=%async_computation.5 | async-start | bytes 1474560
  792.3 1.7 collective-permute-start
  (57 other events, 56.2 us)
Sparse Core Ops, SparseCore 0:
  27.7 245.9 all-gather.3
  693.0 52.7 all-reduce.2
  761.6 27.5 reduce-scatter.3
